TPU v7x, 256 devices: a whole 4x4x8 slice. The times are simulated.
256 devices in a mesh: seq: 64 (over z, y, core), head: 4 (over x).
Axes of the slice: x: 4, y: 4, z: 8, core: 2. Of those that a mesh axis runs over, the one named last changes fastest.
Arguments:
- queries: bfloat16 [32, 64, 128], P(None, 'head'), may hold values from -12 to 12
- keys: bfloat16 [32, 8, 8192, 128], P(None, 'head', 'seq'), may hold values from -6 to 6
- values: bfloat16 [32, 8, 8192, 128], P(None, 'head', 'seq'), may hold values from -6 to 6
- codes: int32 [32, 8, 32, 8192], P(None, 'head', None, 'seq'), may hold values from 0 to 255
- centroids: float32 [8, 4, 32, 256], P('head'), may hold values from -6 to 6
- picks: int32 [32, 8, 64], P(None, 'head'), may hold values from 0 to 511, as said below
- block_len: int32 [32, 512], P(None, 'seq'), may hold values from 1 to 16
- out_weight: bfloat16 [8192, 8192], P('head', 'seq'), may hold values from -0.0625 to 0.0625
Outputs:
- estimates: float32 [32, 8, 512], P(None, 'head', 'seq')
- attended: bfloat16 [64, 4, 1024], P('seq', 'head')
- layer_out: bfloat16 [32, 8192], P('head', 'seq')
Inputs may be any that keep to these rules, and one draw needn't show every extreme that they name: Each row picks[b, h, :] holds 64 different block numbers in no particular order; among the 8 blocks j * 8 to (j + 1) * 8 - 1 of any j at most 4 are picked, and in every row some j has exactly 4.
All inputs are finite; a program needn't handle non-finite values.
Results may differ from a plain program's by a relative error of at most 0.0049.
Values may be sent and summed in bfloat16 or wider, within the bound.
A program may use at most 64 MiB of HBM per device.

v0:
```python
import jax
import jax.numpy as jnp
from jax import lax
from jax.sharding import PartitionSpec as P

NEG = -1e30


def slot_matrix(sel_rows, shard, nblk_dev, capacity):
    local = sel_rows - shard * nblk_dev
    inside = (local >= 0) & (local < nblk_dev)
    hits = (local[:, :, None] == lax.iota(jnp.int32, nblk_dev)[None, None, :]) & inside[:, :, None]
    taken = jnp.sum(hits.astype(jnp.int32), axis=1)
    position = jnp.cumsum(taken, axis=1) - 1
    place = (position[:, None, :] == lax.iota(jnp.int32, capacity)[None, :, None]) & (
        taken[:, None, :] > 0
    )
    return place.astype(jnp.bfloat16)


def attend(query, keys_s, values_s, lens_s):
    pairs, rows, width = keys_s.shape
    head_dim = query.shape[-1]
    block = width // head_dim
    key_rows = keys_s.reshape(pairs, rows * block, head_dim)
    value_rows = values_s.reshape(pairs, rows * block, head_dim)
    score = jnp.einsum(
        "pgd,ptd->pgt", query, key_rows, preferred_element_type=jnp.float32
    ) * head_dim ** (-0.5)
    live = (
        lax.iota(jnp.int32, block).astype(jnp.float32)[None, None, :]
        < lens_s.astype(jnp.float32)[:, :, None]
    )
    live = live.reshape(pairs, 1, rows * block)
    top = jnp.max(jnp.where(live, score, NEG), axis=2)
    weight = jnp.where(live, jnp.exp(score - top[:, :, None]), 0.0)
    total = jnp.sum(weight, axis=2)
    acc = jnp.einsum(
        "pgt,ptd->pgd", weight, value_rows.astype(jnp.float32), precision=lax.Precision.HIGHEST
    )
    return (top, total, acc)


def fold_rows(top, total, acc):
    best = jnp.max(top, axis=0)
    scale = jnp.exp(top - best[None])
    return (best, jnp.sum(total * scale, axis=0), jnp.sum(acc * scale[..., None], axis=0))


def shards(queries, keys, values, codes, centroids, picks, block_len, out_weight):
    batch, kv_local, seq_local, head_dim = keys.shape
    group = queries.shape[1] // kv_local
    nblk_dev = block_len.shape[1]
    block = seq_local // nblk_dev
    capacity = nblk_dev // 2
    pairs = batch * kv_local
    sub = centroids.shape[1]
    nsub = centroids.shape[2]
    cent = centroids.shape[3]
    shard = lax.axis_index("seq")
    query_float = queries.astype(jnp.float32).reshape(batch, kv_local, group, nsub, sub)
    table = jnp.einsum(
        "bhgms,hsmc->bhgmc", query_float, centroids, precision=lax.Precision.HIGHEST
    ) * head_dim ** (-0.5)
    table = table.astype(jnp.bfloat16).reshape(pairs, group, nsub * cent)
    lens_pair = jnp.repeat(block_len, kv_local, axis=0)
    step_rows = 4
    steps_count = pairs // step_rows

    def score_group(carry, items):
        tab, code, lens = items
        onehot = (code[:, :, None, :] == lax.iota(jnp.int32, cent)[None, None, :, None]).astype(
            jnp.bfloat16
        )
        onehot = onehot.reshape(step_rows, nsub * cent, seq_local)
        approx = jnp.einsum("pgk,pkt->pgt", tab, onehot, preferred_element_type=jnp.float32)
        approx = approx.reshape(step_rows, group, nblk_dev, block)
        live = (lax.iota(jnp.int32, block)[None, None, :] < lens[:, :, None])[:, None]
        top = jnp.max(jnp.where(live, approx, NEG), axis=(1, 3))
        mass = jnp.sum(jnp.where(live, jnp.exp(approx - top[:, None, :, None]), 0.0), axis=(1, 3))
        return (carry, top + jnp.log(mass))

    grouped = (
        table.reshape(steps_count, step_rows, group, nsub * cent),
        codes.reshape(steps_count, step_rows, nsub, seq_local),
        lens_pair.reshape(steps_count, step_rows, nblk_dev),
    )
    unused, estimated = lax.scan(score_group, 0, grouped)
    estimates = estimated.reshape(batch, kv_local, nblk_dev)
    sel_rows = picks.reshape(pairs, picks.shape[-1])
    place = slot_matrix(sel_rows, shard, nblk_dev, capacity)
    key_blocks = keys.reshape(pairs, nblk_dev, block * head_dim)
    value_blocks = values.reshape(pairs, nblk_dev, block * head_dim)
    lens_float = lens_pair.astype(jnp.float32)
    query_all = queries.reshape(pairs, group, head_dim)
    own_query = lax.dynamic_slice_in_dim(query_all, shard, 1, 0)
    send_keys = jnp.einsum(
        "pcn,pnd->cpd", place, key_blocks, preferred_element_type=jnp.float32
    ).astype(jnp.bfloat16)
    send_values = jnp.einsum(
        "pcn,pnd->cpd", place, value_blocks, preferred_element_type=jnp.float32
    ).astype(jnp.bfloat16)
    send_lens = jnp.einsum("pcn,pn->cp", place.astype(jnp.float32), lens_float).astype(jnp.bfloat16)
    got_keys = lax.all_to_all(send_keys, "seq", split_axis=1, concat_axis=1, tiled=True)
    got_values = lax.all_to_all(send_values, "seq", split_axis=1, concat_axis=1, tiled=True)
    got_lens = lax.all_to_all(send_lens, "seq", split_axis=1, concat_axis=1, tiled=True)
    count = got_keys.shape[0]
    query_rep = jnp.broadcast_to(own_query, (count, group, head_dim))
    pieces = attend(query_rep, got_keys, got_values, got_lens)
    top, total, acc = fold_rows(pieces[0], pieces[1], pieces[2])
    head_out = (acc / total[..., None]).astype(jnp.bfloat16)
    attended = head_out.reshape(1, 1, group * head_dim)
    flat = head_out.reshape(1, group * head_dim)
    weight_parts = out_weight.reshape(kv_local, group * head_dim, out_weight.shape[1])
    piece = lax.all_gather(flat, "seq", axis=0, tiled=True)
    products = jnp.einsum("ik,hkd->ihd", piece, weight_parts, preferred_element_type=jnp.float32)
    parity = lax.iota(jnp.int32, piece.shape[0]) % kv_local
    select = (parity[:, None] == lax.iota(jnp.int32, kv_local)[None, :]).astype(jnp.float32)
    gathered = jnp.sum(products * select[:, :, None], axis=1)
    per_request = jnp.sum(gathered.reshape(batch, kv_local, out_weight.shape[1]), axis=1)
    layer_out = lax.psum_scatter(per_request, "head", scatter_dimension=0, tiled=True).astype(
        jnp.bfloat16
    )
    return (estimates, attended, layer_out)


def solution(mesh):
    placed = (
        P(None, "head", None),
        P(None, "head", "seq", None),
        P(None, "head", "seq", None),
        P(None, "head", None, "seq"),
        P("head", None, None, None),
        P(None, "head", None),
        P(None, "seq"),
        P("head", "seq"),
    )
    return jax.shard_map(
        shards,
        mesh=mesh,
        in_specs=placed,
        out_specs=(P(None, "head", "seq"), P("seq", "head", None), P("head", "seq")),
        check_vma=False,
    )
```

profile of v0, /device:TPU:8, one launch (start us, length us, event | category | flops | bytes accessed | tf_op | source)
XLA Modules:
  0.0 276.4 jit_solution(5679206314056601219)
XLA Ops:
  4.7 12.1 %all-to-all-start = ((bf16[4,64,1]{0,2,1:T(2,128)(2,1)}), bf16[4,64,1]{0,2,1:T(2,128)(2,1)S(1)}, u32[]{:S(2)}, u32[]{:S(2)}) async-start(bf16[4,64,1]{0,2,1:T(2,128)(2,1)} %copy.64), calls=%async_computation | async-start | bytes 65536 | tf_op jit(solution)/shard_map/all_to_all | solution.py:106
  21.4 4.0 %all-to-all-done = bf16[4,64,1]{0,2,1:T(2,128)(2,1)S(1)} async-done(((bf16[4,64,1]{0,2,1:T(2,128)(2,1)}), bf16[4,64,1]{0,2,1:T(2,128)(2,1)S(1)}, u32[]{:S(2)}, u32[]{:S(2)}) %all-to-all-start) | async-done | bytes 544 | tf_op jit(solution)/shard_map/all_to_all | solution.py:106
  25.5 6.6 %all-to-all-start.1 = ((bf16[4,64,2048]{2,0,1:T(4,128)(2,1)}), bf16[4,64,2048]{2,0,1:T(4,128)(2,1)}, u32[]{:S(2)}, u32[]{:S(2)}) async-start(bf16[4,64,2048]{2,0,1:T(4,128)(2,1)} %fusion.5), calls=%async_computation.1 | async-start | bytes 2097152 | tf_op jit(solution)/shard_map/all_to_all | solution.py:104
  36.4 9.1 %fusion.4 = bf16[32,2,8,32,256]{4,0,2,3,1:T(8,128)(2,1)} fusion(bf16[32,2,8,32,4]{0,2,1,4,3:T(8,128)(2,1)S(1)} %bitcast.87, f32[2,4,32,256,1]{3,2,1,0,4:T(8,128)S(1)} %bitcast.90), kind=kOutput, calls=%fused_computation.13 | convolution fusion | flops 209715200 | bytes 8781824 | tf_op jit(solution)/shard_map/bhgms,hsmc->bhgmc/dot_general | solution.py:62
  45.5 11.4 %copy.62 = bf16[32,2,8,32,256]{4,3,2,1,0:T(8,128)(2,1)} copy(bf16[32,2,8,32,256]{4,0,2,3,1:T(8,128)(2,1)} %fusion.4) | data formatting | bytes 16777216 | tf_op jit(solution)/shard_map/convert_element_type | solution.py:65
  56.9 13.5 %reshape_reshape.7 = bf16[16,4,8,8192]{3,2,1,0:T(8,128)(2,1)} reshape(bf16[32,2,8,32,256]{4,3,2,1,0:T(8,128)(2,1)} %copy.62) | data formatting | bytes 16777216 | tf_op jit(solution)/shard_map/reshape;reshape | solution.py:84
  72.1 10.3 %all-to-all-start.2 = ((bf16[4,64,2048]{2,0,1:T(4,128)(2,1)}), bf16[4,64,2048]{2,0,1:T(4,128)(2,1)S(1)}, u32[]{:S(2)}, u32[]{:S(2)}) async-start(bf16[4,64,2048]{2,0,1:T(4,128)(2,1)} %fusion.6), calls=%async_computation.2 | async-start | bytes 2097152 | tf_op jit(solution)/shard_map/all_to_all | solution.py:105
  82.5 120.3 %while.10 = (s32[]{:T(128)}, f32[16,4,8]{2,1,0:T(4,128)S(1)}, s32[16,4,8]{2,1,0:T(4,128)S(1)}, bf16[16,4,8,8192]{3,2,1,0:T(8,128)(2,1)}, s32[16,4,32,128]{3,2,1,0:T(8,128)}, /*index=5*/s32[]{:T(128)}, f32[]{:T(128)}, f32[]{:T(128)}) while((s32[]{:T(128)}, f32[16,4,8]{2,1,0:T(4,128)S(1)}, s32[16,4,8]{2,1,0:T(4,128)S(1)}, ...), condition=%wide.region_5.6_spmd, body=%wide.region_0.5_spmd.sunk | while | flops 71324128 | bytes 9317225 | solution.py:88
  86.3 3.1 %select_reduce_fusion.6 = (f32[4,128]{1,0:T(4,128)S(1)}, f32[4,8,128]{2,1,0:T(8,128)S(1)}) fusion(pred[4,128]{1,0:T(4,128)(4,1)S(1)} %broadcast_compare_fusion.4, pred[4,8192,128]{2,1,0:T(32,128)(4,1)S(1)} %bitcast_compare_fusion.2, bf16[16,4,8,8192]{3,2,1,0:T(8,128)(2,1)} %get-tuple-element.121, s32[]{:T(128)} %get-tuple-element.110), kind=kOutput, calls=%fused_computation.7.clone.1 | convolution fusion | flops 67116544 | bytes 4738048 | tf_op jit(solution)/shard_map/while/body/eval_jaxpr/pgk,pkt->pgt/dot_general | solution.py:76
  93.8 3.1 %select_reduce_fusion.6 = (f32[4,128]{1,0:T(4,128)S(1)}, f32[4,8,128]{2,1,0:T(8,128)S(1)}) fusion(pred[4,128]{1,0:T(4,128)(4,1)S(1)} %broadcast_compare_fusion.4, pred[4,8192,128]{2,1,0:T(32,128)(4,1)S(1)} %bitcast_compare_fusion.2, bf16[16,4,8,8192]{3,2,1,0:T(8,128)(2,1)} %get-tuple-element.121, s32[]{:T(128)} %get-tuple-element.110), kind=kOutput, calls=%fused_computation.7.clone.1 | convolution fusion | flops 67116544 | bytes 4738048 | tf_op jit(solution)/shard_map/while/body/eval_jaxpr/pgk,pkt->pgt/dot_general | solution.py:76
  101.3 3.1 %select_reduce_fusion.6 = (f32[4,128]{1,0:T(4,128)S(1)}, f32[4,8,128]{2,1,0:T(8,128)S(1)}) fusion(pred[4,128]{1,0:T(4,128)(4,1)S(1)} %broadcast_compare_fusion.4, pred[4,8192,128]{2,1,0:T(32,128)(4,1)S(1)} %bitcast_compare_fusion.2, bf16[16,4,8,8192]{3,2,1,0:T(8,128)(2,1)} %get-tuple-element.121, s32[]{:T(128)} %get-tuple-element.110), kind=kOutput, calls=%fused_computation.7.clone.1 | convolution fusion | flops 67116544 | bytes 4738048 | tf_op jit(solution)/shard_map/while/body/eval_jaxpr/pgk,pkt->pgt/dot_general | solution.py:76
  108.9 3.1 %select_reduce_fusion.6 = (f32[4,128]{1,0:T(4,128)S(1)}, f32[4,8,128]{2,1,0:T(8,128)S(1)}) fusion(pred[4,128]{1,0:T(4,128)(4,1)S(1)} %broadcast_compare_fusion.4, pred[4,8192,128]{2,1,0:T(32,128)(4,1)S(1)} %bitcast_compare_fusion.2, bf16[16,4,8,8192]{3,2,1,0:T(8,128)(2,1)} %get-tuple-element.121, s32[]{:T(128)} %get-tuple-element.110), kind=kOutput, calls=%fused_computation.7.clone.1 | convolution fusion | flops 67116544 | bytes 4738048 | tf_op jit(solution)/shard_map/while/body/eval_jaxpr/pgk,pkt->pgt/dot_general | solution.py:76
  116.4 3.1 %select_reduce_fusion.6 = (f32[4,128]{1,0:T(4,128)S(1)}, f32[4,8,128]{2,1,0:T(8,128)S(1)}) fusion(pred[4,128]{1,0:T(4,128)(4,1)S(1)} %broadcast_compare_fusion.4, pred[4,8192,128]{2,1,0:T(32,128)(4,1)S(1)} %bitcast_compare_fusion.2, bf16[16,4,8,8192]{3,2,1,0:T(8,128)(2,1)} %get-tuple-element.121, s32[]{:T(128)} %get-tuple-element.110), kind=kOutput, calls=%fused_computation.7.clone.1 | convolution fusion | flops 67116544 | bytes 4738048 | tf_op jit(solution)/shard_map/while/body/eval_jaxpr/pgk,pkt->pgt/dot_general | solution.py:76
  123.9 3.1 %select_reduce_fusion.6 = (f32[4,128]{1,0:T(4,128)S(1)}, f32[4,8,128]{2,1,0:T(8,128)S(1)}) fusion(pred[4,128]{1,0:T(4,128)(4,1)S(1)} %broadcast_compare_fusion.4, pred[4,8192,128]{2,1,0:T(32,128)(4,1)S(1)} %bitcast_compare_fusion.2, bf16[16,4,8,8192]{3,2,1,0:T(8,128)(2,1)} %get-tuple-element.121, s32[]{:T(128)} %get-tuple-element.110), kind=kOutput, calls=%fused_computation.7.clone.1 | convolution fusion | flops 67116544 | bytes 4738048 | tf_op jit(solution)/shard_map/while/body/eval_jaxpr/pgk,pkt->pgt/dot_general | solution.py:76
  131.4 3.1 %select_reduce_fusion.6 = (f32[4,128]{1,0:T(4,128)S(1)}, f32[4,8,128]{2,1,0:T(8,128)S(1)}) fusion(pred[4,128]{1,0:T(4,128)(4,1)S(1)} %broadcast_compare_fusion.4, pred[4,8192,128]{2,1,0:T(32,128)(4,1)S(1)} %bitcast_compare_fusion.2, bf16[16,4,8,8192]{3,2,1,0:T(8,128)(2,1)} %get-tuple-element.121, s32[]{:T(128)} %get-tuple-element.110), kind=kOutput, calls=%fused_computation.7.clone.1 | convolution fusion | flops 67116544 | bytes 4738048 | tf_op jit(solution)/shard_map/while/body/eval_jaxpr/pgk,pkt->pgt/dot_general | solution.py:76
  138.9 3.1 %select_reduce_fusion.6 = (f32[4,128]{1,0:T(4,128)S(1)}, f32[4,8,128]{2,1,0:T(8,128)S(1)}) fusion(pred[4,128]{1,0:T(4,128)(4,1)S(1)} %broadcast_compare_fusion.4, pred[4,8192,128]{2,1,0:T(32,128)(4,1)S(1)} %bitcast_compare_fusion.2, bf16[16,4,8,8192]{3,2,1,0:T(8,128)(2,1)} %get-tuple-element.121, s32[]{:T(128)} %get-tuple-element.110), kind=kOutput, calls=%fused_computation.7.clone.1 | convolution fusion | flops 67116544 | bytes 4738048 | tf_op jit(solution)/shard_map/while/body/eval_jaxpr/pgk,pkt->pgt/dot_general | solution.py:76
  146.5 3.1 %select_reduce_fusion.6 = (f32[4,128]{1,0:T(4,128)S(1)}, f32[4,8,128]{2,1,0:T(8,128)S(1)}) fusion(pred[4,128]{1,0:T(4,128)(4,1)S(1)} %broadcast_compare_fusion.4, pred[4,8192,128]{2,1,0:T(32,128)(4,1)S(1)} %bitcast_compare_fusion.2, bf16[16,4,8,8192]{3,2,1,0:T(8,128)(2,1)} %get-tuple-element.121, s32[]{:T(128)} %get-tuple-element.110), kind=kOutput, calls=%fused_computation.7.clone.1 | convolution fusion | flops 67116544 | bytes 4738048 | tf_op jit(solution)/shard_map/while/body/eval_jaxpr/pgk,pkt->pgt/dot_general | solution.py:76
  154.0 3.1 %select_reduce_fusion.6 = (f32[4,128]{1,0:T(4,128)S(1)}, f32[4,8,128]{2,1,0:T(8,128)S(1)}) fusion(pred[4,128]{1,0:T(4,128)(4,1)S(1)} %broadcast_compare_fusion.4, pred[4,8192,128]{2,1,0:T(32,128)(4,1)S(1)} %bitcast_compare_fusion.2, bf16[16,4,8,8192]{3,2,1,0:T(8,128)(2,1)} %get-tuple-element.121, s32[]{:T(128)} %get-tuple-element.110), kind=kOutput, calls=%fused_computation.7.clone.1 | convolution fusion | flops 67116544 | bytes 4738048 | tf_op jit(solution)/shard_map/while/body/eval_jaxpr/pgk,pkt->pgt/dot_general | solution.py:76
  161.5 3.1 %select_reduce_fusion.6 = (f32[4,128]{1,0:T(4,128)S(1)}, f32[4,8,128]{2,1,0:T(8,128)S(1)}) fusion(pred[4,128]{1,0:T(4,128)(4,1)S(1)} %broadcast_compare_fusion.4, pred[4,8192,128]{2,1,0:T(32,128)(4,1)S(1)} %bitcast_compare_fusion.2, bf16[16,4,8,8192]{3,2,1,0:T(8,128)(2,1)} %get-tuple-element.121, s32[]{:T(128)} %get-tuple-element.110), kind=kOutput, calls=%fused_computation.7.clone.1 | convolution fusion | flops 67116544 | bytes 4738048 | tf_op jit(solution)/shard_map/while/body/eval_jaxpr/pgk,pkt->pgt/dot_general | solution.py:76
  169.0 3.1 %select_reduce_fusion.6 = (f32[4,128]{1,0:T(4,128)S(1)}, f32[4,8,128]{2,1,0:T(8,128)S(1)}) fusion(pred[4,128]{1,0:T(4,128)(4,1)S(1)} %broadcast_compare_fusion.4, pred[4,8192,128]{2,1,0:T(32,128)(4,1)S(1)} %bitcast_compare_fusion.2, bf16[16,4,8,8192]{3,2,1,0:T(8,128)(2,1)} %get-tuple-element.121, s32[]{:T(128)} %get-tuple-element.110), kind=kOutput, calls=%fused_computation.7.clone.1 | convolution fusion | flops 67116544 | bytes 4738048 | tf_op jit(solution)/shard_map/while/body/eval_jaxpr/pgk,pkt->pgt/dot_general | solution.py:76
  176.5 3.1 %select_reduce_fusion.6 = (f32[4,128]{1,0:T(4,128)S(1)}, f32[4,8,128]{2,1,0:T(8,128)S(1)}) fusion(pred[4,128]{1,0:T(4,128)(4,1)S(1)} %broadcast_compare_fusion.4, pred[4,8192,128]{2,1,0:T(32,128)(4,1)S(1)} %bitcast_compare_fusion.2, bf16[16,4,8,8192]{3,2,1,0:T(8,128)(2,1)} %get-tuple-element.121, s32[]{:T(128)} %get-tuple-element.110), kind=kOutput, calls=%fused_computation.7.clone.1 | convolution fusion | flops 67116544 | bytes 4738048 | tf_op jit(solution)/shard_map/while/body/eval_jaxpr/pgk,pkt->pgt/dot_general | solution.py:76
  191.6 3.1 %select_reduce_fusion.6 = (f32[4,128]{1,0:T(4,128)S(1)}, f32[4,8,128]{2,1,0:T(8,128)S(1)}) fusion(pred[4,128]{1,0:T(4,128)(4,1)S(1)} %broadcast_compare_fusion.4, pred[4,8192,128]{2,1,0:T(32,128)(4,1)S(1)} %bitcast_compare_fusion.2, bf16[16,4,8,8192]{3,2,1,0:T(8,128)(2,1)} %get-tuple-element.121, s32[]{:T(128)} %get-tuple-element.110), kind=kOutput, calls=%fused_computation.7.clone.1 | convolution fusion | flops 67116544 | bytes 4738048 | tf_op jit(solution)/shard_map/while/body/eval_jaxpr/pgk,pkt->pgt/dot_general | solution.py:76
  214.7 43.9 %all-gather = bf16[64,1,1024]{2,1,0:T(2,128)(2,1)S(1)} all-gather(bf16[1,1,1024]{2,1,0:T(2,128)(2,1)S(1)} %convert_element_type.94), channel_id=1, replica_groups=mesh['seq'=64,'head'=4] {'seq'}, dimensions={0}, use_global_device_ids=true | all-gather | bytes 133120 | tf_op jit(solution)/shard_map/all_gather | solution.py:115
  258.9 16.9 %all-reduce = bf16[32,128]{1,0:T(8,128)(2,1)S(1)} all-reduce(f32[32,128]{1,0:T(8,128)S(1)} %reduce_sum.75), channel_id=2, replica_groups=mesh['seq'=64,'head'=4] {'head'}, use_global_device_ids=true, to_apply=%region_15.16.clone | all-reduce | flops 4096 | bytes 24576
  (350 shorter events, 102.4 us)
Async XLA Ops:
  0.6 258.0 %copy-start = (bf16[2048,128]{1,0:T(8,128)(2,1)S(1)}, bf16[2048,128]{1,0:T(8,128)(2,1)}, u32[]{:S(2)}) copy-start(bf16[2048,128]{1,0:T(8,128)(2,1)} %param.17) | copy-start | bytes 1572868
  4.7 20.7 %all-to-all-start = ((bf16[4,64,1]{0,2,1:T(2,128)(2,1)}), bf16[4,64,1]{0,2,1:T(2,128)(2,1)S(1)}, u32[]{:S(2)}, u32[]{:S(2)}) async-start(bf16[4,64,1]{0,2,1:T(2,128)(2,1)} %copy.64), calls=%async_computation | async-start | bytes 65536 | tf_op jit(solution)/shard_map/all_to_all | solution.py:106
  16.8 15.2 %copy-start.3 = (s32[32,8]{0,1:T(8,128)S(1)}, s32[32,8]{0,1:T(8,128)}, u32[]{:S(2)}) copy-start(s32[32,8]{0,1:T(8,128)} %param.16) | copy-start | bytes 3076
  21.4 15.0 %copy-start.1 = (f32[2,4,32,256]{3,2,1,0:T(8,128)S(1)}, f32[2,4,32,256]{3,2,1,0:T(8,128)}, u32[]{:S(2)}) copy-start(f32[2,4,32,256]{3,2,1,0:T(8,128)} %param.14) | copy-start | bytes 786436
  25.5 46.7 %all-to-all-start.1 = ((bf16[4,64,2048]{2,0,1:T(4,128)(2,1)}), bf16[4,64,2048]{2,0,1:T(4,128)(2,1)}, u32[]{:S(2)}, u32[]{:S(2)}) async-start(bf16[4,64,2048]{2,0,1:T(4,128)(2,1)} %fusion.5), calls=%async_computation.1 | async-start | bytes 2097152 | tf_op jit(solution)/shard_map/all_to_all | solution.py:104
  72.1 138.0 %all-to-all-start.2 = ((bf16[4,64,2048]{2,0,1:T(4,128)(2,1)}), bf16[4,64,2048]{2,0,1:T(4,128)(2,1)S(1)}, u32[]{:S(2)}, u32[]{:S(2)}) async-start(bf16[4,64,2048]{2,0,1:T(4,128)(2,1)} %fusion.6), calls=%async_computation.2 | async-start | bytes 2097152 | tf_op jit(solution)/shard_map/all_to_all | solution.py:105
  82.5 121.1 %copy-start.4 = (u32[256]{0:T(256)S(1)}, u32[256]{0:T(256)}, u32[]{:S(2)}) copy-start(u32[256]{0:T(256)} %constant.73) | copy-start | bytes 3076
  214.7 61.7 %copy-start.2 = (bf16[1,1,1024]{2,1,0:T(2,128)(2,1)}, bf16[1,1,1024]{2,1,0:T(2,128)(2,1)S(1)}, u32[]{:S(2)}) copy-start(bf16[1,1,1024]{2,1,0:T(2,128)(2,1)S(1)} %convert_element_type.94) | copy-start | bytes 6148
where the time goes:
time: 279 us; the launch traced here: 276 us
  local copies, waits for them, and re-layouts  66.1 us (24%)
  matrix products  64.2 us (23%)
  blocking collectives  60.9 us (22%)
  other arithmetic  49.9 us (18%)
  starting transfers between devices  29 us (10%)
  waiting for transfers between devices  4.04 us (1%)
    dot_general x16, matrix products, score_group(): jnp.einsum('pgk,pkt->pgt', tab, onehot, preferred_element_type=jnp.float32)  50.1 us
    all_gather x1, blocking collectives, shards(): piece = lax.all_gather(flat, 'seq', axis=0, tiled=True)  43.9 us
    eq x16, other arithmetic, score_group(): code[:, :, None, :] == lax.iota(jnp.int32, cent)[None, None, :, None]  42.6 us
    unnamed x1, blocking collectives  16.9 us
    eq x16, local copies, waits for them, and re-layouts, score_group(): code[:, :, None, :] == lax.iota(jnp.int32, cent)[None, None, :, None]  13.6 us
    another operation x1, local copies, waits for them, and re-layouts, shards(): table.reshape(steps_count, step_rows, group, nsub * cent)  13.5 us
    all_to_all x1, starting transfers between devices, shards(): lax.all_to_all(send_lens, 'seq', split_axis=1, concat_axis=1, tiled=True)  12.1 us
    convert_element_type x1, local copies, waits for them, and re-layouts, shards(): table = table.astype(jnp.bfloat16).reshape(pairs, group, nsub * cent)  11.4 us
  transfers between devices with their start and end apart: 3, of which 1 were waited for; matrix products, arithmetic and copies ran while one was open for 62% of the time, Pallas kernels for 0%

commit v1 on v0

--- a/solution.py
+++ b/solution.py
@@ -112,7 +112,9 @@
     attended = head_out.reshape(1, 1, group * head_dim)
     flat = head_out.reshape(1, group * head_dim)
     weight_parts = out_weight.reshape(kv_local, group * head_dim, out_weight.shape[1])
-    piece = lax.all_gather(flat, "seq", axis=0, tiled=True)
+    piece = jnp.concatenate(
+        lax.all_to_all(jnp.stack([flat] * lax.axis_size("seq")), "seq", 0, 0), axis=0
+    )
     products = jnp.einsum("ik,hkd->ihd", piece, weight_parts, preferred_element_type=jnp.float32)
     parity = lax.iota(jnp.int32, piece.shape[0]) % kv_local
     select = (parity[:, None] == lax.iota(jnp.int32, kv_local)[None, :]).astype(jnp.float32)

time: 279 us -> 256 us (0.918)
  blocking collectives: 60.9 us -> 16.9 us
  starting transfers between devices: 29 us -> 39.3 us
  waiting for transfers between devices: 4.04 us -> 11.4 us
    all_gather x1 -> x0, blocking collectives: 43.9 us -> none  [shards(): piece = lax.all_gather(flat, 'seq', axis=0, tiled=True)]
    all_to_all x0 -> x1, starting transfers between devices: none -> 10.3 us  [shards(): lax.all_to_all(jnp.stack([flat] * lax.axis_size('seq')), 'seq', 0, 0)]
    all_to_all x0 -> x1, waiting for transfers between devices: none -> 7.31 us  [shards(): lax.all_to_all(jnp.stack([flat] * lax.axis_size('seq')), 'seq', 0, 0)]
  transfers between devices with their start and end apart: 3 -> 4, of which waited for: 1 -> 2; matrix products, arithmetic and copies ran while one was open for 62% -> 68% of each run, Pallas kernels for 0% -> 0%
where the time goes in v1:
time: 256 us; the launch traced here: 254 us
  local copies, waits for them, and re-layouts  68.2 us (27%)
  matrix products  64.2 us (25%)
  other arithmetic  51.4 us (20%)
  starting transfers between devices  39.3 us (15%)
  blocking collectives  16.9 us (7%)
  waiting for transfers between devices  11.4 us (4%)
    dot_general x16, matrix products, score_group(): jnp.einsum('pgk,pkt->pgt', tab, onehot, preferred_element_type=jnp.float32)  50.1 us
    eq x16, other arithmetic, score_group(): code[:, :, None, :] == lax.iota(jnp.int32, cent)[None, None, :, None]  42.6 us
    unnamed x1, blocking collectives  16.9 us
    eq x16, local copies, waits for them, and re-layouts, score_group(): code[:, :, None, :] == lax.iota(jnp.int32, cent)[None, None, :, None]  13.6 us
    another operation x1, local copies, waits for them, and re-layouts, shards(): table.reshape(steps_count, step_rows, group, nsub * cent)  13.5 us
    all_to_all x1, starting transfers between devices, shards(): lax.all_to_all(send_lens, 'seq', split_axis=1, concat_axis=1, tiled=True)  12.1 us
    convert_element_type x1, local copies, waits for them, and re-layouts, shards(): table = table.astype(jnp.bfloat16).reshape(pairs, group, nsub * cent)  11.4 us
    all_to_all x1, starting transfers between devices, shards(): lax.all_to_all(send_values, 'seq', split_axis=1, concat_axis=1, tiled=True)  10.3 us
  transfers between devices with their start and end apart: 4, of which 2 were waited for; matrix products, arithmetic and copies ran while one was open for 68% of the time, Pallas kernels for 0%

profile of v1, /device:TPU:8, one launch (start us, length us, event | category | flops | bytes accessed | tf_op | source)
XLA Modules:
  0.0 253.6 jit_solution(2183667334936739245)
XLA Ops:
  4.7 12.1 %all-to-all-start = ((bf16[4,64,1]{0,2,1:T(2,128)(2,1)}), bf16[4,64,1]{0,2,1:T(2,128)(2,1)S(1)}, u32[]{:S(2)}, u32[]{:S(2)}) async-start(bf16[4,64,1]{0,2,1:T(2,128)(2,1)} %copy.62), calls=%async_computation | async-start | bytes 65536 | tf_op jit(solution)/shard_map/all_to_all | solution.py:106
  21.4 4.0 %all-to-all-done = bf16[4,64,1]{0,2,1:T(2,128)(2,1)S(1)} async-done(((bf16[4,64,1]{0,2,1:T(2,128)(2,1)}), bf16[4,64,1]{0,2,1:T(2,128)(2,1)S(1)}, u32[]{:S(2)}, u32[]{:S(2)}) %all-to-all-start) | async-done | bytes 544 | tf_op jit(solution)/shard_map/all_to_all | solution.py:106
  25.5 6.6 %all-to-all-start.1 = ((bf16[4,64,2048]{2,0,1:T(4,128)(2,1)}), bf16[4,64,2048]{2,0,1:T(4,128)(2,1)}, u32[]{:S(2)}, u32[]{:S(2)}) async-start(bf16[4,64,2048]{2,0,1:T(4,128)(2,1)} %fusion.5), calls=%async_computation.1 | async-start | bytes 2097152 | tf_op jit(solution)/shard_map/all_to_all | solution.py:104
  36.4 9.1 %fusion.4 = bf16[32,2,8,32,256]{4,0,2,3,1:T(8,128)(2,1)} fusion(bf16[32,2,8,32,4]{0,2,1,4,3:T(8,128)(2,1)S(1)} %bitcast.89, f32[2,4,32,256,1]{3,2,1,0,4:T(8,128)S(1)} %bitcast.92), kind=kOutput, calls=%fused_computation.13 | convolution fusion | flops 209715200 | bytes 8781824 | tf_op jit(solution)/shard_map/bhgms,hsmc->bhgmc/dot_general | solution.py:62
  45.5 11.4 %copy.60 = bf16[32,2,8,32,256]{4,3,2,1,0:T(8,128)(2,1)} copy(bf16[32,2,8,32,256]{4,0,2,3,1:T(8,128)(2,1)} %fusion.4) | data formatting | bytes 16777216 | tf_op jit(solution)/shard_map/convert_element_type | solution.py:65
  56.9 13.5 %reshape_reshape.7 = bf16[16,4,8,8192]{3,2,1,0:T(8,128)(2,1)} reshape(bf16[32,2,8,32,256]{4,3,2,1,0:T(8,128)(2,1)} %copy.60) | data formatting | bytes 16777216 | tf_op jit(solution)/shard_map/reshape;reshape | solution.py:84
  72.1 10.3 %all-to-all-start.2 = ((bf16[4,64,2048]{2,0,1:T(4,128)(2,1)}), bf16[4,64,2048]{2,0,1:T(4,128)(2,1)S(1)}, u32[]{:S(2)}, u32[]{:S(2)}) async-start(bf16[4,64,2048]{2,0,1:T(4,128)(2,1)} %fusion.6), calls=%async_computation.2 | async-start | bytes 2097152 | tf_op jit(solution)/shard_map/all_to_all | solution.py:105
  82.5 120.3 %while.10 = (s32[]{:T(128)}, f32[16,4,8]{2,1,0:T(4,128)S(1)}, s32[16,4,8]{2,1,0:T(4,128)S(1)}, bf16[16,4,8,8192]{3,2,1,0:T(8,128)(2,1)}, s32[16,4,32,128]{3,2,1,0:T(8,128)}, /*index=5*/s32[]{:T(128)}, f32[]{:T(128)}, f32[]{:T(128)}) while((s32[]{:T(128)}, f32[16,4,8]{2,1,0:T(4,128)S(1)}, s32[16,4,8]{2,1,0:T(4,128)S(1)}, ...), condition=%wide.region_5.6_spmd, body=%wide.region_0.5_spmd.sunk | while | flops 71324128 | bytes 9317225 | solution.py:88
  86.3 3.1 %select_reduce_fusion.6 = (f32[4,128]{1,0:T(4,128)S(1)}, f32[4,8,128]{2,1,0:T(8,128)S(1)}) fusion(pred[4,128]{1,0:T(4,128)(4,1)S(1)} %broadcast_compare_fusion.4, pred[4,8192,128]{2,1,0:T(32,128)(4,1)S(1)} %bitcast_compare_fusion.2, bf16[16,4,8,8192]{3,2,1,0:T(8,128)(2,1)} %get-tuple-element.118, s32[]{:T(128)} %get-tuple-element.107), kind=kOutput, calls=%fused_computation.7.clone.1 | convolution fusion | flops 67116544 | bytes 4738048 | tf_op jit(solution)/shard_map/while/body/eval_jaxpr/pgk,pkt->pgt/dot_general | solution.py:76
  93.8 3.1 %select_reduce_fusion.6 = (f32[4,128]{1,0:T(4,128)S(1)}, f32[4,8,128]{2,1,0:T(8,128)S(1)}) fusion(pred[4,128]{1,0:T(4,128)(4,1)S(1)} %broadcast_compare_fusion.4, pred[4,8192,128]{2,1,0:T(32,128)(4,1)S(1)} %bitcast_compare_fusion.2, bf16[16,4,8,8192]{3,2,1,0:T(8,128)(2,1)} %get-tuple-element.118, s32[]{:T(128)} %get-tuple-element.107), kind=kOutput, calls=%fused_computation.7.clone.1 | convolution fusion | flops 67116544 | bytes 4738048 | tf_op jit(solution)/shard_map/while/body/eval_jaxpr/pgk,pkt->pgt/dot_general | solution.py:76
  101.3 3.1 %select_reduce_fusion.6 = (f32[4,128]{1,0:T(4,128)S(1)}, f32[4,8,128]{2,1,0:T(8,128)S(1)}) fusion(pred[4,128]{1,0:T(4,128)(4,1)S(1)} %broadcast_compare_fusion.4, pred[4,8192,128]{2,1,0:T(32,128)(4,1)S(1)} %bitcast_compare_fusion.2, bf16[16,4,8,8192]{3,2,1,0:T(8,128)(2,1)} %get-tuple-element.118, s32[]{:T(128)} %get-tuple-element.107), kind=kOutput, calls=%fused_computation.7.clone.1 | convolution fusion | flops 67116544 | bytes 4738048 | tf_op jit(solution)/shard_map/while/body/eval_jaxpr/pgk,pkt->pgt/dot_general | solution.py:76
  108.9 3.1 %select_reduce_fusion.6 = (f32[4,128]{1,0:T(4,128)S(1)}, f32[4,8,128]{2,1,0:T(8,128)S(1)}) fusion(pred[4,128]{1,0:T(4,128)(4,1)S(1)} %broadcast_compare_fusion.4, pred[4,8192,128]{2,1,0:T(32,128)(4,1)S(1)} %bitcast_compare_fusion.2, bf16[16,4,8,8192]{3,2,1,0:T(8,128)(2,1)} %get-tuple-element.118, s32[]{:T(128)} %get-tuple-element.107), kind=kOutput, calls=%fused_computation.7.clone.1 | convolution fusion | flops 67116544 | bytes 4738048 | tf_op jit(solution)/shard_map/while/body/eval_jaxpr/pgk,pkt->pgt/dot_general | solution.py:76
  116.4 3.1 %select_reduce_fusion.6 = (f32[4,128]{1,0:T(4,128)S(1)}, f32[4,8,128]{2,1,0:T(8,128)S(1)}) fusion(pred[4,128]{1,0:T(4,128)(4,1)S(1)} %broadcast_compare_fusion.4, pred[4,8192,128]{2,1,0:T(32,128)(4,1)S(1)} %bitcast_compare_fusion.2, bf16[16,4,8,8192]{3,2,1,0:T(8,128)(2,1)} %get-tuple-element.118, s32[]{:T(128)} %get-tuple-element.107), kind=kOutput, calls=%fused_computation.7.clone.1 | convolution fusion | flops 67116544 | bytes 4738048 | tf_op jit(solution)/shard_map/while/body/eval_jaxpr/pgk,pkt->pgt/dot_general | solution.py:76
  123.9 3.1 %select_reduce_fusion.6 = (f32[4,128]{1,0:T(4,128)S(1)}, f32[4,8,128]{2,1,0:T(8,128)S(1)}) fusion(pred[4,128]{1,0:T(4,128)(4,1)S(1)} %broadcast_compare_fusion.4, pred[4,8192,128]{2,1,0:T(32,128)(4,1)S(1)} %bitcast_compare_fusion.2, bf16[16,4,8,8192]{3,2,1,0:T(8,128)(2,1)} %get-tuple-element.118, s32[]{:T(128)} %get-tuple-element.107), kind=kOutput, calls=%fused_computation.7.clone.1 | convolution fusion | flops 67116544 | bytes 4738048 | tf_op jit(solution)/shard_map/while/body/eval_jaxpr/pgk,pkt->pgt/dot_general | solution.py:76
  131.4 3.1 %select_reduce_fusion.6 = (f32[4,128]{1,0:T(4,128)S(1)}, f32[4,8,128]{2,1,0:T(8,128)S(1)}) fusion(pred[4,128]{1,0:T(4,128)(4,1)S(1)} %broadcast_compare_fusion.4, pred[4,8192,128]{2,1,0:T(32,128)(4,1)S(1)} %bitcast_compare_fusion.2, bf16[16,4,8,8192]{3,2,1,0:T(8,128)(2,1)} %get-tuple-element.118, s32[]{:T(128)} %get-tuple-element.107), kind=kOutput, calls=%fused_computation.7.clone.1 | convolution fusion | flops 67116544 | bytes 4738048 | tf_op jit(solution)/shard_map/while/body/eval_jaxpr/pgk,pkt->pgt/dot_general | solution.py:76
  138.9 3.1 %select_reduce_fusion.6 = (f32[4,128]{1,0:T(4,128)S(1)}, f32[4,8,128]{2,1,0:T(8,128)S(1)}) fusion(pred[4,128]{1,0:T(4,128)(4,1)S(1)} %broadcast_compare_fusion.4, pred[4,8192,128]{2,1,0:T(32,128)(4,1)S(1)} %bitcast_compare_fusion.2, bf16[16,4,8,8192]{3,2,1,0:T(8,128)(2,1)} %get-tuple-element.118, s32[]{:T(128)} %get-tuple-element.107), kind=kOutput, calls=%fused_computation.7.clone.1 | convolution fusion | flops 67116544 | bytes 4738048 | tf_op jit(solution)/shard_map/while/body/eval_jaxpr/pgk,pkt->pgt/dot_general | solution.py:76
  146.4 3.1 %select_reduce_fusion.6 = (f32[4,128]{1,0:T(4,128)S(1)}, f32[4,8,128]{2,1,0:T(8,128)S(1)}) fusion(pred[4,128]{1,0:T(4,128)(4,1)S(1)} %broadcast_compare_fusion.4, pred[4,8192,128]{2,1,0:T(32,128)(4,1)S(1)} %bitcast_compare_fusion.2, bf16[16,4,8,8192]{3,2,1,0:T(8,128)(2,1)} %get-tuple-element.118, s32[]{:T(128)} %get-tuple-element.107), kind=kOutput, calls=%fused_computation.7.clone.1 | convolution fusion | flops 67116544 | bytes 4738048 | tf_op jit(solution)/shard_map/while/body/eval_jaxpr/pgk,pkt->pgt/dot_general | solution.py:76
  154.0 3.1 %select_reduce_fusion.6 = (f32[4,128]{1,0:T(4,128)S(1)}, f32[4,8,128]{2,1,0:T(8,128)S(1)}) fusion(pred[4,128]{1,0:T(4,128)(4,1)S(1)} %broadcast_compare_fusion.4, pred[4,8192,128]{2,1,0:T(32,128)(4,1)S(1)} %bitcast_compare_fusion.2, bf16[16,4,8,8192]{3,2,1,0:T(8,128)(2,1)} %get-tuple-element.118, s32[]{:T(128)} %get-tuple-element.107), kind=kOutput, calls=%fused_computation.7.clone.1 | convolution fusion | flops 67116544 | bytes 4738048 | tf_op jit(solution)/shard_map/while/body/eval_jaxpr/pgk,pkt->pgt/dot_general | solution.py:76
  161.5 3.1 %select_reduce_fusion.6 = (f32[4,128]{1,0:T(4,128)S(1)}, f32[4,8,128]{2,1,0:T(8,128)S(1)}) fusion(pred[4,128]{1,0:T(4,128)(4,1)S(1)} %broadcast_compare_fusion.4, pred[4,8192,128]{2,1,0:T(32,128)(4,1)S(1)} %bitcast_compare_fusion.2, bf16[16,4,8,8192]{3,2,1,0:T(8,128)(2,1)} %get-tuple-element.118, s32[]{:T(128)} %get-tuple-element.107), kind=kOutput, calls=%fused_computation.7.clone.1 | convolution fusion | flops 67116544 | bytes 4738048 | tf_op jit(solution)/shard_map/while/body/eval_jaxpr/pgk,pkt->pgt/dot_general | solution.py:76
  169.0 3.1 %select_reduce_fusion.6 = (f32[4,128]{1,0:T(4,128)S(1)}, f32[4,8,128]{2,1,0:T(8,128)S(1)}) fusion(pred[4,128]{1,0:T(4,128)(4,1)S(1)} %broadcast_compare_fusion.4, pred[4,8192,128]{2,1,0:T(32,128)(4,1)S(1)} %bitcast_compare_fusion.2, bf16[16,4,8,8192]{3,2,1,0:T(8,128)(2,1)} %get-tuple-element.118, s32[]{:T(128)} %get-tuple-element.107), kind=kOutput, calls=%fused_computation.7.clone.1 | convolution fusion | flops 67116544 | bytes 4738048 | tf_op jit(solution)/shard_map/while/body/eval_jaxpr/pgk,pkt->pgt/dot_general | solution.py:76
  176.5 3.1 %select_reduce_fusion.6 = (f32[4,128]{1,0:T(4,128)S(1)}, f32[4,8,128]{2,1,0:T(8,128)S(1)}) fusion(pred[4,128]{1,0:T(4,128)(4,1)S(1)} %broadcast_compare_fusion.4, pred[4,8192,128]{2,1,0:T(32,128)(4,1)S(1)} %bitcast_compare_fusion.2, bf16[16,4,8,8192]{3,2,1,0:T(8,128)(2,1)} %get-tuple-element.118, s32[]{:T(128)} %get-tuple-element.107), kind=kOutput, calls=%fused_computation.7.clone.1 | convolution fusion | flops 67116544 | bytes 4738048 | tf_op jit(solution)/shard_map/while/body/eval_jaxpr/pgk,pkt->pgt/dot_general | solution.py:76
  215.5 10.3 %all-to-all-start.3 = ((bf16[64,2,512]{2,1,0:T(2,128)(2,1)}), bf16[64,2,512]{2,1,0:T(2,128)(2,1)S(1)}, u32[]{:S(2)}, u32[]{:S(2)}) async-start(bf16[64,2,512]{2,1,0:T(2,128)(2,1)} %reshape.228), calls=%async_computation.3 | async-start | bytes 262144 | tf_op jit(solution)/shard_map/all_to_all | solution.py:116
  228.4 7.3 %all-to-all-done.3 = bf16[64,2,512]{2,1,0:T(2,128)(2,1)S(1)} async-done(((bf16[64,2,512]{2,1,0:T(2,128)(2,1)}), bf16[64,2,512]{2,1,0:T(2,128)(2,1)S(1)}, u32[]{:S(2)}, u32[]{:S(2)}) %all-to-all-start.3) | async-done | bytes 131104 | tf_op jit(solution)/shard_map/all_to_all | solution.py:116
  236.1 16.9 %all-reduce = bf16[32,128]{1,0:T(8,128)(2,1)S(1)} all-reduce(f32[32,128]{1,0:T(8,128)S(1)} %reduce_sum.75), channel_id=2, replica_groups=mesh['seq'=64,'head'=4] {'head'}, use_global_device_ids=true, to_apply=%region_15.16.clone | all-reduce | flops 4096 | bytes 24576
  (355 shorter events, 109.1 us)
Async XLA Ops:
  0.6 235.2 %copy-start = (bf16[2048,128]{1,0:T(8,128)(2,1)S(1)}, bf16[2048,128]{1,0:T(8,128)(2,1)}, u32[]{:S(2)}) copy-start(bf16[2048,128]{1,0:T(8,128)(2,1)} %param.17) | copy-start | bytes 1572868
  4.7 20.7 %all-to-all-start = ((bf16[4,64,1]{0,2,1:T(2,128)(2,1)}), bf16[4,64,1]{0,2,1:T(2,128)(2,1)S(1)}, u32[]{:S(2)}, u32[]{:S(2)}) async-start(bf16[4,64,1]{0,2,1:T(2,128)(2,1)} %copy.62), calls=%async_computation | async-start | bytes 65536 | tf_op jit(solution)/shard_map/all_to_all | solution.py:106
  16.8 15.2 %copy-start.2 = (s32[32,8]{0,1:T(8,128)S(1)}, s32[32,8]{0,1:T(8,128)}, u32[]{:S(2)}) copy-start(s32[32,8]{0,1:T(8,128)} %param.16) | copy-start | bytes 3076
  21.4 15.0 %copy-start.1 = (f32[2,4,32,256]{3,2,1,0:T(8,128)S(1)}, f32[2,4,32,256]{3,2,1,0:T(8,128)}, u32[]{:S(2)}) copy-start(f32[2,4,32,256]{3,2,1,0:T(8,128)} %param.14) | copy-start | bytes 786436
  25.5 46.7 %all-to-all-start.1 = ((bf16[4,64,2048]{2,0,1:T(4,128)(2,1)}), bf16[4,64,2048]{2,0,1:T(4,128)(2,1)}, u32[]{:S(2)}, u32[]{:S(2)}) async-start(bf16[4,64,2048]{2,0,1:T(4,128)(2,1)} %fusion.5), calls=%async_computation.1 | async-start | bytes 2097152 | tf_op jit(solution)/shard_map/all_to_all | solution.py:104
  72.1 136.1 %all-to-all-start.2 = ((bf16[4,64,2048]{2,0,1:T(4,128)(2,1)}), bf16[4,64,2048]{2,0,1:T(4,128)(2,1)S(1)}, u32[]{:S(2)}, u32[]{:S(2)}) async-start(bf16[4,64,2048]{2,0,1:T(4,128)(2,1)} %fusion.6), calls=%async_computation.2 | async-start | bytes 2097152 | tf_op jit(solution)/shard_map/all_to_all | solution.py:105
  208.3 18.3 %copy-start.3 = (u32[256]{0:T(256)S(1)}, u32[256]{0:T(256)}, u32[]{:S(2)}) copy-start(u32[256]{0:T(256)} %constant.73) | copy-start | bytes 3076
  215.5 20.2 %all-to-all-start.3 = ((bf16[64,2,512]{2,1,0:T(2,128)(2,1)}), bf16[64,2,512]{2,1,0:T(2,128)(2,1)S(1)}, u32[]{:S(2)}, u32[]{:S(2)}) async-start(bf16[64,2,512]{2,1,0:T(2,128)(2,1)} %reshape.228), calls=%async_computation.3 | async-start | bytes 262144 | tf_op jit(solution)/shard_map/all_to_all | solution.py:116
